TPU v7x, 512 devices: a whole 4x8x8 slice. The times are simulated.
512 devices in a mesh: imp: 32 (over z, x), adv: 16 (over y, core).
Axes of the slice: x: 4, y: 8, z: 8, core: 2. Of those that a mesh axis runs over, the one named last changes fastest.
Arguments:
- impression_vectors: bfloat16 [64, 65536], P(None, 'imp'), may hold values from -6 to 6
- advertiser_vectors: bfloat16 [64, 65536], P(None, ('imp', 'adv')), may hold values from -0.75 to 0.75
- spend_limits: float32 [65536], P(('imp', 'adv')), may hold values from 1024 to 8192
- capacity: float32 [65536], P('imp'), may hold values from 1024 to 8192
- blocks: int32 [512, 16, 8], P('imp', 'adv'), may hold values from 0 to 511, as said below
- counts: int32 [512, 16], P('imp', 'adv'), may hold values from 1 to 8, as said below
Outputs:
- prices: float32 [65536], P(('imp', 'adv'))
- impression_duals: float32 [65536], P('imp')
- impression_grad: bfloat16 [64, 65536], P(None, ('imp', 'adv'))
- advertiser_grad: bfloat16 [64, 65536], P(None, ('imp', 'adv'))
Inputs may be any that keep to these rules, and one draw needn't show every extreme that they name: Block numbers. Entry [g, a, k] names a block b with (b) % (the size of adv) == a. The 8 entries of one list are distinct; entries at slots k >= counts[g, a] are padding and name valid blocks too. `counts`: every group has one index of adv whose count is 8.
All inputs are finite; a program needn't handle non-finite values.
Results may differ from a plain program's by a relative error of at most 0.012.
Values may be sent and summed in bfloat16 or wider, within the bound.
No kernel may reach another device: no remote copies, remote signals or barrier semaphores. Data moves between devices by JAX's collectives and lax.ppermute only.
A program may use at most 64 MiB of HBM per device.

v0:
```python
import jax
import jax.numpy as jnp
from jax import lax
from jax.sharding import PartitionSpec as P

GROUP = 128
BLOCK = 128
ITERS = 3
BLK_DEV = 1


def local(impression_vectors, advertiser_vectors, spend_limits, capacity, blocks, counts):
    features = impression_vectors.shape[0]
    groups_here = blocks.shape[0]
    slot_count = blocks.shape[2]
    adv_devices = lax.axis_size("adv")
    block_ids = blocks.reshape(groups_here, slot_count)
    local_ids = block_ids // BLK_DEV // adv_devices * BLK_DEV + block_ids % BLK_DEV
    live_slots = (jnp.arange(slot_count)[None, :] < counts).astype(jnp.float32)
    viewers = impression_vectors.reshape(features, groups_here, GROUP)
    extent = slot_count * BLOCK
    own_count = spend_limits.shape[0]
    fetched = lax.all_gather(advertiser_vectors, "imp", axis=1, tiled=True)
    catalog = fetched.reshape(features, fetched.shape[1] // BLOCK, BLOCK)
    local_blocks = catalog.shape[1]

    def allocate(source, prices, duals, group_no):
        chosen = lax.dynamic_index_in_dim(local_ids, group_no, 0, keepdims=False)
        columns = jnp.take(source, chosen, axis=1).reshape(features, extent)
        viewer = lax.dynamic_index_in_dim(viewers, group_no, 1, keepdims=False)
        scores = lax.dot_general(
            viewer, columns, (((0,), (0,)), ((), ())), preferred_element_type=jnp.float32
        )
        charged = jnp.take(prices, chosen, axis=0).reshape(extent)
        shadow = lax.dynamic_slice_in_dim(duals, group_no * GROUP, GROUP)
        eligible = jnp.repeat(
            lax.dynamic_index_in_dim(live_slots, group_no, 0, keepdims=False), BLOCK
        )
        shares = jnp.clip(scores - charged[None, :] - shadow[:, None], 0.0, 1.0) * eligible[None, :]
        return (shares, chosen, columns, viewer)

    duals = jnp.zeros((groups_here * GROUP,), jnp.float32)
    range_prices = jnp.zeros((local_blocks, BLOCK), jnp.float32)
    own_prices = jnp.zeros((own_count,), jnp.float32)
    for iteration in range(ITERS):
        totals_prices = range_prices

        def advance(group_no, pair):
            outlay, demand = pair
            shares, chosen, _, _ = allocate(catalog, totals_prices, duals, group_no)
            outlay = outlay.at[chosen].add(jnp.sum(shares, axis=0).reshape(slot_count, BLOCK))
            demand = lax.dynamic_update_slice_in_dim(
                demand, jnp.sum(shares, axis=1), group_no * GROUP, 0
            )
            return (outlay, demand)

        totals_start = (
            jnp.zeros((local_blocks, BLOCK), jnp.float32),
            jnp.zeros((groups_here * GROUP,), jnp.float32),
        )
        outlay, demand = lax.fori_loop(0, groups_here, advance, totals_start)
        own_outlay = lax.psum_scatter(outlay.reshape(-1), "imp", scatter_dimension=0, tiled=True)
        dual_demand = demand
        dual_demand = lax.psum(dual_demand, "adv")
        duals = jnp.maximum(duals + dual_demand / capacity - 1.0, 0.0)
        own_prices = jnp.maximum(own_prices + own_outlay / spend_limits - 1.0, 0.0)
        range_prices = lax.all_gather(own_prices, "imp", axis=0, tiled=True).reshape(
            local_blocks, BLOCK
        )

    def grad_step(group_no, pair):
        imp_part, adv_part = pair
        shares, chosen, columns, viewer = allocate(catalog, range_prices, duals, group_no)
        weights = shares.astype(jnp.bfloat16)
        imp_cols = lax.dot_general(
            columns, weights, (((1,), (1,)), ((), ())), preferred_element_type=jnp.float32
        )
        imp_part = lax.dynamic_update_slice_in_dim(imp_part, imp_cols, group_no * GROUP, 1)
        adv_terms = jnp.dot(viewer, weights, preferred_element_type=jnp.float32).reshape(
            features, slot_count, BLOCK
        )
        adv_part = adv_part.at[:, chosen].add(adv_terms)
        return (imp_part, adv_part)

    start = (
        jnp.zeros((features, groups_here * GROUP), jnp.float32),
        jnp.zeros((features, local_blocks, BLOCK), jnp.float32),
    )
    imp_part, adv_part = lax.fori_loop(0, groups_here, grad_step, start)
    impression_grad = lax.psum_scatter(imp_part, "adv", scatter_dimension=1, tiled=True).astype(
        jnp.bfloat16
    )
    adv_rounded = (adv_part.reshape(features, -1) / GROUP).astype(jnp.bfloat16)
    advertiser_grad = (
        lax.psum_scatter(adv_rounded, "imp", scatter_dimension=1, tiled=True)
        .astype(jnp.float32)
        .astype(jnp.bfloat16)
    )
    return (own_prices, duals, impression_grad, advertiser_grad)


def solution(mesh):
    return jax.shard_map(
        local,
        mesh=mesh,
        in_specs=(
            P(None, "imp"),
            P(None, ("imp", "adv")),
            P(("imp", "adv")),
            P("imp"),
            P("imp", "adv", None),
            P("imp", "adv"),
        ),
        out_specs=(P(("imp", "adv")), P("imp"), P(None, ("imp", "adv")), P(None, ("imp", "adv"))),
        check_vma=False,
    )
```

profile of v0, /device:TPU:25, one launch (start us, length us, event | category | flops | bytes accessed | tf_op | source)
XLA Modules:
  0.0 1180.3 jit_solution(11911110707107156288)
XLA Ops:
  9.5 44.2 %all_gather.12 = bf16[64,4096]{1,0:T(8,128)(2,1)S(1)} all-gather(bf16[64,128]{1,0:T(8,128)(2,1)S(1)} %copy-done.7), channel_id=1, replica_groups=mesh['imp'=32,'adv'=16] {'imp'}, dimensions={1}, use_global_device_ids=true | all-gather | bytes 540672 | tf_op jit(solution)/shard_map/all_gather | solution.py:23
  53.8 41.5 %while.60 = (s32[]{:T(128)}, f32[32,128]{1,0:T(8,128)S(1)}, f32[2048]{0:T(1024)S(1)}, s32[16,8]{1,0:T(8,128)S(1)}, bf16[64,16,128]{2,0,1:T(8,128)(2,1)S(1)}, /*i...) while((s32[]{:T(128)}, f32[32,128]{1,0:T(8,128)S(1)}, ...), condition=%wide.region_4.7_spmd, body=%wide.region_0.6_spmd.sunk | while | flops 17500104 | bytes 485907 | solution.py:61
  95.4 35.8 %psum.21 = f32[2048]{0:T(1024)S(1)} all-reduce(f32[2048]{0:T(1024)S(1)} %get-tuple-element.597), channel_id=1, replica_groups=mesh['imp'=32,'adv'=16] {'adv'}, use_global_device_ids=true, to_apply=%region_6.9 | all-reduce | flops 2048 | bytes 16384 | tf_op jit(solution)/shard_map/psum | solution.py:64
  131.2 112.5 %all-reduce = f32[4096]{0:T(1024)S(1)} all-reduce(f32[4096]{0:T(1024)S(1)} %bitcast.255), channel_id=2, replica_groups=mesh['imp'=32,'adv'=16] {'imp'}, use_global_device_ids=true, to_apply=%region_5.8.clone | all-reduce | flops 4096 | bytes 32768
  243.8 1.3 dynamic-slice
  245.8 28.0 %all-gather = f32[32,1,128]{2,1,0:T(1,128)S(1)} all-gather(f32[1,1,128]{2,1,0:T(1,128)S(1)} %bitcast.260), channel_id=1, replica_groups=mesh['imp'=32,'adv'=16] {'imp'}, dimensions={0}, use_global_device_ids=true | all-gather | bytes 16896 | tf_op jit(solution)/shard_map/all_gather | solution.py:67
  273.8 42.5 %while.61 = (s32[]{:T(128)}, f32[32,128]{1,0:T(8,128)S(1)}, f32[2048]{0:T(1024)S(1)}, s32[16,8]{1,0:T(8,128)S(1)}, bf16[64,16,128]{2,0,1:T(8,128)(2,1)S(1)}, /*i...) while((s32[]{:T(128)}, f32[32,128]{1,0:T(8,128)S(1)}, ...), condition=%wide.region_11.14_spmd, body=%wide.region_7.13_spmd.sunk | while | flops 17631180 | bytes 471067 | solution.py:61
  316.3 58.5 %psum.22 = f32[2048]{0:T(1024)S(1)} all-reduce(f32[2048]{0:T(1024)S(1)} %get-tuple-element.599), channel_id=1, replica_groups=mesh['imp'=32,'adv'=16] {'adv'}, use_global_device_ids=true, to_apply=%region_13.16 | all-reduce | flops 2048 | bytes 16384 | tf_op jit(solution)/shard_map/psum | solution.py:64
  374.8 112.3 %all-reduce.1 = f32[4096]{0:T(1024)S(1)} all-reduce(f32[4096]{0:T(1024)S(1)} %bitcast.256), channel_id=3, replica_groups=mesh['imp'=32,'adv'=16] {'imp'}, use_global_device_ids=true, to_apply=%region_12.15.clone | all-reduce | flops 4096 | bytes 32768
  487.2 27.5 %all-gather.1 = f32[32,1,128]{2,1,0:T(1,128)S(1)} all-gather(f32[1,1,128]{2,1,0:T(1,128)S(1)} %bitcast.259), channel_id=1, replica_groups=mesh['imp'=32,'adv'=16] {'imp'}, dimensions={0}, use_global_device_ids=true | all-gather | bytes 16896 | tf_op jit(solution)/shard_map/all_gather | solution.py:67
  514.7 42.4 %while.62 = (s32[]{:T(128)}, f32[32,128]{1,0:T(8,128)S(1)}, f32[2048]{0:T(1024)S(1)}, s32[16,8]{1,0:T(8,128)S(1)}, bf16[64,16,128]{2,0,1:T(8,128)(2,1)S(1)}, /*i...) while((s32[]{:T(128)}, f32[32,128]{1,0:T(8,128)S(1)}, ...), condition=%wide.region_18.21_spmd, body=%wide.region_14.20_spmd.sunk | while | flops 17631180 | bytes 471067 | solution.py:61
  557.1 59.3 %psum.23 = f32[2048]{0:T(1024)S(1)} all-reduce(f32[2048]{0:T(1024)S(1)} %get-tuple-element.601), channel_id=1, replica_groups=mesh['imp'=32,'adv'=16] {'adv'}, use_global_device_ids=true, to_apply=%region_20.23 | all-reduce | flops 2048 | bytes 16384 | tf_op jit(solution)/shard_map/psum | solution.py:64
  617.1 111.9 %all-reduce.2 = f32[4096]{0:T(1024)S(1)} all-reduce(f32[4096]{0:T(1024)S(1)} %bitcast.257), channel_id=4, replica_groups=mesh['imp'=32,'adv'=16] {'imp'}, use_global_device_ids=true, to_apply=%region_19.22.clone | all-reduce | flops 4096 | bytes 32768
  729.6 27.5 %all-gather.2 = f32[32,1,128]{2,1,0:T(1,128)S(1)} all-gather(f32[1,1,128]{2,1,0:T(1,128)S(1)} %bitcast.261), channel_id=1, replica_groups=mesh['imp'=32,'adv'=16] {'imp'}, dimensions={0}, use_global_device_ids=true | all-gather | bytes 16896 | tf_op jit(solution)/shard_map/all_gather | solution.py:67
  757.2 95.1 %while.63 = (s32[]{:T(128)}, f32[64,2048]{1,0:T(8,128)S(1)}, f32[64,32,128]{2,0,1:T(8,128)S(1)}, s32[16,8]{1,0:T(8,128)S(1)}, bf16[64,32,128]{2,0,1:T(8,128)(2,1...) while((s32[]{:T(128)}, f32[64,2048]{1,0:T(8,128)S(1)}, ...), condition=%wide.region_23.26_spmd, body=%wide.region_21.25_spmd.sunk | while | flops 51185740 | bytes 2993603 | solution.py:89
  757.8 0.8 dynamic_slice.201
  762.2 0.9 scatter_fusion
  763.7 0.8 dynamic_slice.201
  768.2 0.9 scatter_fusion
  769.7 0.8 dynamic_slice.201
  774.1 0.9 scatter_fusion
  775.6 0.8 dynamic_slice.201
  780.0 0.9 scatter_fusion
  781.6 0.8 dynamic_slice.201
  786.0 0.9 scatter_fusion
  787.5 0.8 dynamic_slice.201
  791.9 0.9 scatter_fusion
  793.5 0.8 dynamic_slice.201
  797.9 0.9 scatter_fusion
  799.4 0.8 dynamic_slice.201
  803.8 0.9 scatter_fusion
  805.4 0.8 dynamic_slice.201
  809.8 0.9 scatter_fusion
  811.3 0.8 dynamic_slice.201
  815.7 0.9 scatter_fusion
  821.7 0.9 scatter_fusion
  823.2 0.8 dynamic_slice.201
  827.6 0.9 scatter_fusion
  833.6 0.9 scatter_fusion
  839.5 0.9 scatter_fusion
  841.0 0.8 dynamic_slice.201
  845.4 0.9 scatter_fusion
  851.4 0.9 scatter_fusion
  853.1 1.3 copy.68
  855.3 250.8 %reduce-scatter.7.cloned.1.call-done = bf16[128,64]{1,0:T(8,128)(2,1)} async-done(((bf16[4096,64]{1,0:T(8,128)(2,1)}), bf16[128,64]{1,0:T(8,128)(2,1)}) %reduce-scatter.7.cloned.1.call-update) | async-done | bytes 16400
  1106.1 1.4 copy.67
  1107.5 64.6 %reduce-scatter.5.cloned.1.call-done = f32[64,128]{1,0:T(8,128)} async-done(((f32[64,2048]{1,0:T(8,128)}), f32[64,128]{1,0:T(8,128)}) %reduce-scatter.5.cloned.1.call-update) | async-done | bytes 32784 | tf_op jit(solution)/shard_map/reduce_scatter | solution.py:90
  1172.1 1.4 convert_element_type.23
  (972 shorter events, 198.5 us)
Async XLA Ops:
  7.2 1.6 copy-start
  7.2 1098.9 %reduce-scatter.7.cloned.1.call-start = ((), (), s32[]{:S(2)}) async-start(), calls=%async_computation.3 | async-start | bytes 1081344
  245.8 28.0 %copy-start.2 = (f32[2048]{0:T(1024)S(1)}, f32[2048]{0:T(1024)}, u32[]{:S(2)}) copy-start(f32[2048]{0:T(1024)} %param.21) | copy-start | bytes 24580
  757.2 2.0 copy-start.5
  759.2 1.2 copy-start.3
  762.2 0.9 copy-start.10
  763.1 2.0 copy-start.5
  765.1 1.2 copy-start.3
  768.2 0.9 copy-start.10
  769.1 2.0 copy-start.5
  771.1 1.2 copy-start.3
  774.1 0.9 copy-start.10
  775.0 2.0 copy-start.5
  777.0 1.2 copy-start.3
  780.0 0.9 copy-start.10
  781.0 2.0 copy-start.5
  783.0 1.2 copy-start.3
  786.0 0.9 copy-start.10
  786.9 2.0 copy-start.5
  788.9 1.2 copy-start.3
  791.9 0.9 copy-start.10
  792.9 2.0 copy-start.5
  794.8 1.2 copy-start.3
  797.9 0.9 copy-start.10
  798.8 2.0 copy-start.5
  800.8 1.2 copy-start.3
  803.8 0.9 copy-start.10
  804.8 2.0 copy-start.5
  806.7 1.2 copy-start.3
  809.8 0.9 copy-start.10
  810.7 2.0 copy-start.5
  812.7 1.2 copy-start.3
  815.7 0.9 copy-start.10
  816.7 2.0 copy-start.5
  818.6 1.2 copy-start.3
  821.7 0.9 copy-start.10
  822.6 2.0 copy-start.5
  824.6 1.2 copy-start.3
  827.6 0.9 copy-start.10
  828.5 2.0 copy-start.5
  830.5 1.2 copy-start.3
  834.5 2.0 copy-start.5
  836.5 1.2 copy-start.3
  840.4 2.0 copy-start.5
  842.4 1.2 copy-start.3
  846.4 2.0 copy-start.5
  848.4 1.2 copy-start.3
  854.5 317.6 %reduce-scatter.5.cloned.1.call-start = ((), (), s32[]{:S(2)}) async-start(), calls=%async_computation.2 | async-start | bytes 557056 | tf_op jit(solution)/shard_map/reduce_scatter | solution.py:90
  (74 other events, 52.7 us)
Sparse Core Ops, SparseCore 0:
  854.6 251.3 reduce-scatter.6
  1108.8 63.2 reduce-scatter.4
where the time goes:
time: 1180 us
  blocking collectives  617 us (52%)
  waiting for transfers between devices  316 us (27%)
  local copies, waits for them, and re-layouts  133 us (11%)
  other arithmetic  62.3 us (5%)
  matrix products  30.7 us (3%)
  between operations  14.9 us (1%)
    unnamed x3, blocking collectives  337 us
    unnamed x3, waiting for transfers between devices  252 us
    psum x3, blocking collectives, local(): dual_demand = lax.psum(dual_demand, 'adv')  154 us
    all_gather x3, blocking collectives, local(): lax.all_gather(own_prices, 'imp', axis=0, tiled=True)  83 us
    reduce_scatter x1, waiting for transfers between devices, local(): lax.psum_scatter(imp_part, 'adv', scatter_dimension=1, tiled=True)  64.6 us
    all_gather x1, blocking collectives, local(): fetched = lax.all_gather(advertiser_vectors, 'imp', axis=1, tiled=True)  44.2 us
    gather x64, local copies, waits for them, and re-layouts, allocate(): columns = jnp.take(source, chosen, axis=1).reshape(features, extent)  36.6 us
    gather x64, local copies, waits for them, and re-layouts, allocate(): charged = jnp.take(prices, chosen, axis=0).reshape(extent)  35.6 us
  transfers between devices with their start and end apart: 2, of which 2 were waited for; matrix products, arithmetic and copies ran while one was open for 0% of the time, Pallas kernels for 0%

commit v1 on v0

--- a/solution.py
+++ b/solution.py
@@ -2,6 +2,7 @@
 import jax.numpy as jnp
 from jax import lax
 from jax.sharding import PartitionSpec as P
+from jax.lax import all_to_all, psum
 
 GROUP = 128
 BLOCK = 128
@@ -64,9 +65,16 @@
         dual_demand = lax.psum(dual_demand, "adv")
         duals = jnp.maximum(duals + dual_demand / capacity - 1.0, 0.0)
         own_prices = jnp.maximum(own_prices + own_outlay / spend_limits - 1.0, 0.0)
-        range_prices = lax.all_gather(own_prices, "imp", axis=0, tiled=True).reshape(
-            local_blocks, BLOCK
+        remake_matrix_here = lambda field_in: jnp.concatenate(
+            all_to_all(
+                jnp.stack([field_in for _ in range(psum(1, axis_name="imp"))]),
+                axis_name="imp",
+                split_axis=0,
+                concat_axis=0,
+            ),
+            axis=0,
         )
+        range_prices = remake_matrix_here(own_prices).reshape(local_blocks, BLOCK)
 
     def grad_step(group_no, pair):
         imp_part, adv_part = pair

time: 1180 us -> 1110 us (0.941)
  blocking collectives: 617 us -> 524 us
  starting transfers between devices: 0.08 us -> 12.5 us
    all_gather x3 -> x0, blocking collectives: 83 us -> none  [local(): lax.all_gather(own_prices, 'imp', axis=0, tiled=True)]
    all_to_all x0 -> x3, waiting for transfers between devices: none -> 16.4 us  [local(): all_to_all(jnp.stack([field_in for _ in range(psum(1, axis_name='imp'))])...]
    all_to_all x0 -> x3, starting transfers between devices: none -> 12.4 us  [local(): all_to_all(jnp.stack([field_in for _ in range(psum(1, axis_name='imp'))])...]
    psum x3, blocking collectives: 154 us -> 141 us  [local(): dual_demand = lax.psum(dual_demand, 'adv')]
  transfers between devices with their start and end apart: 2 -> 5, of which waited for: 2 -> 4; matrix products, arithmetic and copies ran while one was open for 0% -> 0% of each run, Pallas kernels for 0% -> 0%
where the time goes in v1:
time: 1110 us
  blocking collectives  524 us (47%)
  waiting for transfers between devices  323 us (29%)
  local copies, waits for them, and re-layouts  135 us (12%)
  other arithmetic  62.3 us (6%)
  matrix products  30.7 us (3%)
  between operations  14.9 us (1%)
  starting transfers between devices  12.5 us (1%)
    unnamed x3, blocking collectives  339 us
    unnamed x3, waiting for transfers between devices  242 us
    psum x3, blocking collectives, local(): dual_demand = lax.psum(dual_demand, 'adv')  141 us
    reduce_scatter x1, waiting for transfers between devices, local(): lax.psum_scatter(imp_part, 'adv', scatter_dimension=1, tiled=True)  64.6 us
    all_gather x1, blocking collectives, local(): fetched = lax.all_gather(advertiser_vectors, 'imp', axis=1, tiled=True)  44.2 us
    gather x64, local copies, waits for them, and re-layouts, allocate(): columns = jnp.take(source, chosen, axis=1).reshape(features, extent)  36.6 us
    gather x64, local copies, waits for them, and re-layouts, allocate(): charged = jnp.take(prices, chosen, axis=0).reshape(extent)  35.6 us
    scatter-add x48, other arithmetic, advance(): outlay.at[chosen].add(jnp.sum(shares, axis=0).reshape(slot_count, BLOCK))  29.9 us
  transfers between devices with their start and end apart: 5, of which 4 were waited for; matrix products, arithmetic and copies ran while one was open for 0% of the time, Pallas kernels for 0%

profile of v1, /device:TPU:25, one launch (start us, length us, event | category | flops | bytes accessed | tf_op | source)
XLA Modules:
  0.0 1107.5 jit_solution(7616647094819972915)
XLA Ops:
  9.4 44.2 %all_gather.3 = bf16[64,4096]{1,0:T(8,128)(2,1)S(1)} all-gather(bf16[64,128]{1,0:T(8,128)(2,1)S(1)} %copy-done.7), channel_id=1, replica_groups=mesh['imp'=32,'adv'=16] {'imp'}, dimensions={1}, use_global_device_ids=true | all-gather | bytes 540672 | tf_op jit(solution)/shard_map/all_gather | solution.py:24
  53.8 41.5 %while.60 = (s32[]{:T(128)}, f32[32,128]{1,0:T(8,128)S(1)}, f32[2048]{0:T(1024)S(1)}, s32[16,8]{1,0:T(8,128)S(1)}, bf16[64,16,128]{2,0,1:T(8,128)(2,1)S(1)}, /*i...) while((s32[]{:T(128)}, f32[32,128]{1,0:T(8,128)S(1)}, ...), condition=%wide.region_4.7_spmd, body=%wide.region_0.6_spmd.sunk | while | flops 17500104 | bytes 485907 | solution.py:62
  95.3 112.7 %all-reduce = f32[4096]{0:T(1024)S(1)} all-reduce(f32[4096]{0:T(1024)S(1)} %bitcast.252), channel_id=2, replica_groups=mesh['imp'=32,'adv'=16] {'imp'}, use_global_device_ids=true, to_apply=%region_5.8.clone | all-reduce | flops 4096 | bytes 32768
  208.0 1.3 dynamic-slice
  210.7 3.8 all-to-all-start
  214.5 64.0 %psum.21 = f32[2048]{0:T(1024)S(1)} all-reduce(f32[2048]{0:T(1024)S(1)} %get-tuple-element.597), channel_id=1, replica_groups=mesh['imp'=32,'adv'=16] {'adv'}, use_global_device_ids=true, to_apply=%region_6.9 | all-reduce | flops 2048 | bytes 16384 | tf_op jit(solution)/shard_map/psum | solution.py:65
  278.6 42.5 %while.61 = (s32[]{:T(128)}, f32[32,128]{1,0:T(8,128)S(1)}, f32[2048]{0:T(1024)S(1)}, s32[16,8]{1,0:T(8,128)S(1)}, bf16[64,16,128]{2,0,1:T(8,128)(2,1)S(1)}, /*i...) while((s32[]{:T(128)}, f32[32,128]{1,0:T(8,128)S(1)}, ...), condition=%wide.region_11.14_spmd, body=%wide.region_7.13_spmd.sunk | while | flops 17631180 | bytes 471067 | solution.py:62
  321.1 24.1 %psum.22 = f32[2048]{0:T(1024)S(1)} all-reduce(f32[2048]{0:T(1024)S(1)} %get-tuple-element.599), channel_id=1, replica_groups=mesh['imp'=32,'adv'=16] {'adv'}, use_global_device_ids=true, to_apply=%region_13.16 | all-reduce | flops 2048 | bytes 16384 | tf_op jit(solution)/shard_map/psum | solution.py:65
  345.2 115.0 %all-reduce.1 = f32[4096]{0:T(1024)S(1)} all-reduce(f32[4096]{0:T(1024)S(1)} %bitcast.253), channel_id=3, replica_groups=mesh['imp'=32,'adv'=16] {'imp'}, use_global_device_ids=true, to_apply=%region_12.15.clone | all-reduce | flops 4096 | bytes 32768
  460.8 4.4 all-to-all-start.1
  465.3 8.5 all-to-all-done.1
  473.8 42.5 %while.62 = (s32[]{:T(128)}, f32[32,128]{1,0:T(8,128)S(1)}, f32[2048]{0:T(1024)S(1)}, s32[16,8]{1,0:T(8,128)S(1)}, bf16[64,16,128]{2,0,1:T(8,128)(2,1)S(1)}, /*i...) while((s32[]{:T(128)}, f32[32,128]{1,0:T(8,128)S(1)}, ...), condition=%wide.region_18.21_spmd, body=%wide.region_14.20_spmd.sunk | while | flops 17631180 | bytes 471067 | solution.py:62
  516.3 53.3 %psum.23 = f32[2048]{0:T(1024)S(1)} all-reduce(f32[2048]{0:T(1024)S(1)} %get-tuple-element.601), channel_id=1, replica_groups=mesh['imp'=32,'adv'=16] {'adv'}, use_global_device_ids=true, to_apply=%region_20.23 | all-reduce | flops 2048 | bytes 16384 | tf_op jit(solution)/shard_map/psum | solution.py:65
  569.6 111.1 %all-reduce.2 = f32[4096]{0:T(1024)S(1)} all-reduce(f32[4096]{0:T(1024)S(1)} %bitcast.254), channel_id=4, replica_groups=mesh['imp'=32,'adv'=16] {'imp'}, use_global_device_ids=true, to_apply=%region_19.22.clone | all-reduce | flops 4096 | bytes 32768
  681.4 4.2 all-to-all-start.2
  686.2 7.9 all-to-all-done.2
  694.3 95.1 %while.63 = (s32[]{:T(128)}, f32[64,2048]{1,0:T(8,128)S(1)}, f32[64,32,128]{2,0,1:T(8,128)S(1)}, s32[16,8]{1,0:T(8,128)S(1)}, bf16[64,32,128]{2,0,1:T(8,128)(2,1...) while((s32[]{:T(128)}, f32[64,2048]{1,0:T(8,128)S(1)}, ...), condition=%wide.region_23.26_spmd, body=%wide.region_21.25_spmd.sunk | while | flops 51185740 | bytes 2993603 | solution.py:97
  694.9 0.8 dynamic_slice.201
  699.3 0.9 scatter_fusion
  700.8 0.8 dynamic_slice.201
  705.2 0.9 scatter_fusion
  706.8 0.8 dynamic_slice.201
  711.2 0.9 scatter_fusion
  712.7 0.8 dynamic_slice.201
  717.1 0.9 scatter_fusion
  718.7 0.8 dynamic_slice.201
  723.1 0.9 scatter_fusion
  724.6 0.8 dynamic_slice.201
  729.0 0.9 scatter_fusion
  730.6 0.8 dynamic_slice.201
  735.0 0.9 scatter_fusion
  736.5 0.8 dynamic_slice.201
  740.9 0.9 scatter_fusion
  746.9 0.9 scatter_fusion
  752.8 0.9 scatter_fusion
  754.3 0.8 dynamic_slice.201
  758.8 0.9 scatter_fusion
  764.7 0.9 scatter_fusion
  770.6 0.9 scatter_fusion
  772.2 0.8 dynamic_slice.201
  776.6 0.9 scatter_fusion
  782.5 0.9 scatter_fusion
  788.5 0.9 scatter_fusion
  790.2 1.3 copy.68
  792.3 240.9 %reduce-scatter.7.cloned.1.call-done = bf16[128,64]{1,0:T(8,128)(2,1)} async-done(((bf16[4096,64]{1,0:T(8,128)(2,1)}), bf16[128,64]{1,0:T(8,128)(2,1)}) %reduce-scatter.7.cloned.1.call-update) | async-done | bytes 16400
  1033.3 1.4 copy.67
  1034.7 64.6 %reduce-scatter.5.cloned.1.call-done = f32[64,128]{1,0:T(8,128)} async-done(((f32[64,2048]{1,0:T(8,128)}), f32[64,128]{1,0:T(8,128)}) %reduce-scatter.5.cloned.1.call-update) | async-done | bytes 32784 | tf_op jit(solution)/shard_map/reduce_scatter | solution.py:98
  1099.3 1.4 convert_element_type.23
  (978 shorter events, 201.5 us)
Async XLA Ops:
  7.2 1.6 copy-start
  210.7 67.9 %all-to-all-start = ((f32[32,1,128]{2,1,0:T(1,128)}), f32[32,1,128]{2,1,0:T(1,128)S(1)}, u32[]{:S(2)}, u32[]{:S(2)}) async-start(f32[32,1,128]{2,1,0:T(1,128)} %stack.6), calls=%async_computation | async-start | bytes 32768 | tf_op jit(solution)/shard_map/all_to_all | solution.py:69
  214.5 64.1 %copy-start.2 = (f32[2048]{0:T(1024)S(1)}, f32[2048]{0:T(1024)}, u32[]{:S(2)}) copy-start(f32[2048]{0:T(1024)} %param.21) | copy-start | bytes 24580
  460.8 12.9 %all-to-all-start.1 = ((f32[32,1,128]{2,1,0:T(1,128)}), f32[32,1,128]{2,1,0:T(1,128)S(1)}, u32[]{:S(2)}, u32[]{:S(2)}) async-start(f32[32,1,128]{2,1,0:T(1,128)} %stack.7), calls=%async_computation.1 | async-start | bytes 32768 | tf_op jit(solution)/shard_map/all_to_all | solution.py:69
  681.4 12.7 %all-to-all-start.2 = ((f32[32,1,128]{2,1,0:T(1,128)}), f32[32,1,128]{2,1,0:T(1,128)S(1)}, u32[]{:S(2)}, u32[]{:S(2)}) async-start(f32[32,1,128]{2,1,0:T(1,128)} %stack.8), calls=%async_computation.2 | async-start | bytes 32768 | tf_op jit(solution)/shard_map/all_to_all | solution.py:69
  685.6 347.7 %reduce-scatter.7.cloned.1.call-start = ((), (), s32[]{:S(2)}) async-start(), calls=%async_computation.6 | async-start | bytes 1081344
  694.3 2.0 copy-start.5
  696.3 1.2 copy-start.3
  699.3 0.9 copy-start.10
  700.2 2.0 copy-start.5
  702.2 1.2 copy-start.3
  705.2 0.9 copy-start.10
  706.2 2.0 copy-start.5
  708.1 1.2 copy-start.3
  711.2 0.9 copy-start.10
  712.1 2.0 copy-start.5
  714.1 1.2 copy-start.3
  717.1 0.9 copy-start.10
  718.1 2.0 copy-start.5
  720.0 1.2 copy-start.3
  723.1 0.9 copy-start.10
  724.0 2.0 copy-start.5
  726.0 1.2 copy-start.3
  729.0 0.9 copy-start.10
  730.0 2.0 copy-start.5
  731.9 1.2 copy-start.3
  735.0 0.9 copy-start.10
  735.9 2.0 copy-start.5
  737.9 1.2 copy-start.3
  740.9 0.9 copy-start.10
  741.9 2.0 copy-start.5
  743.8 1.2 copy-start.3
  746.9 0.9 copy-start.10
  747.8 2.0 copy-start.5
  749.8 1.2 copy-start.3
  753.7 2.0 copy-start.5
  755.7 1.2 copy-start.3
  759.7 2.0 copy-start.5
  761.7 1.2 copy-start.3
  765.6 2.0 copy-start.5
  767.6 1.2 copy-start.3
  771.6 2.0 copy-start.5
  773.5 1.2 copy-start.3
  777.5 2.0 copy-start.5
  779.5 1.2 copy-start.3
  783.5 2.0 copy-start.5
  785.4 1.2 copy-start.3
  791.6 307.7 %reduce-scatter.5.cloned.1.call-start = ((), (), s32[]{:S(2)}) async-start(), calls=%async_computation.5 | async-start | bytes 557056 | tf_op jit(solution)/shard_map/reduce_scatter | solution.py:98
  (77 other events, 55.6 us)
Sparse Core Ops, SparseCore 0:
  791.7 241.5 reduce-scatter.6
  1036.0 63.1 reduce-scatter.4
